TPU v7x, 256 devices: a whole 4x4x8 slice. The times are simulated.
256 devices in a mesh: frame: 32 (over z_lo, y, core), row: 8 (over x, z_hi).
Axes of the slice: x: 4, y: 4, z: 8 (z_hi: 2, z_lo: 4; z = z_hi * 4 + z_lo), core: 2. Of those that a mesh axis runs over, the one named last changes fastest.
Arguments:
- spatial_q: bfloat16 [32, 1024, 3072], P('frame', 'row'), may hold values from -6 to 6
- spatial_k: bfloat16 [32, 1024, 3072], P('frame', 'row'), may hold values from -6 to 6
- spatial_v: bfloat16 [32, 1024, 3072], P('frame', 'row'), may hold values from -6 to 6
- norm_gain: float32 [3072], replicated, may hold values from 0.5 to 1.5
- temporal_weight: bfloat16 [3072, 3, 3072], P(None, None, 'row'), may hold values from -0.625 to 0.625
Outputs:
- temporal_out: bfloat16 [32, 1024, 3072], P('frame', 'row')
All inputs are finite; a program needn't handle non-finite values.
Results may differ from a plain program's by a relative error of at most 0.0083.
Values may be sent and summed in bfloat16 or wider, within the bound.
A program may use at most 64 MiB of HBM per device.

v0:
```python
import jax
import jax.numpy as jnp
from jax import lax
from jax.sharding import PartitionSpec as P

D = 3072
HEADS = 24
AGENTS = 128


epsilon = 1e-06


def laid_out(tiles, dim):
    tiles = jnp.moveaxis(tiles, 0, dim)
    shape = tiles.shape
    return tiles.reshape(*shape[:dim], shape[dim] * shape[dim + 1], *shape[dim + 2 :])


def from_everyone(x, axis):
    size = lax.axis_size(axis)
    return lax.all_to_all(jnp.broadcast_to(x[None], (size, *x.shape)), axis, 0, 0, tiled=True)


def gather_directly(x, axis, dim):
    return laid_out(from_everyone(x, axis), dim)


def taken_together(x, axis):
    everything = from_everyone(x, axis)
    return jnp.max(everything, axis=0)


def split_up(x, dim, size):
    before, after = (x.shape[:dim], x.shape[dim + 1 :])
    return jnp.moveaxis(x.reshape(*before, size, -1, *after), dim, 0)


def sent_and_summed(x, axis, dim):
    tiles = split_up(x, dim, lax.axis_size(axis))
    arrived = lax.all_to_all(tiles, axis, split_axis=0, concat_axis=0, tiled=True)
    return arrived.sum(axis=0)


def in_one_piece(arrays, axis, dim, along):
    columns = [a.reshape(*a.shape[:along], -1) for a in arrays]
    both = jnp.concatenate(columns, axis=along)
    whole, at, outs = (sent_and_summed(both, axis, dim), 0, [])
    for a, column in zip(arrays, columns):
        piece = whole[..., at : at + column.shape[along]]
        outs.append(piece.reshape(*piece.shape[:along], *a.shape[along:]))
        at += column.shape[along]
    return tuple(outs)


def local(spatial_q, spatial_k, spatial_v, norm_gain, temporal_weight):
    frame_count = lax.axis_size("frame")
    row_count = lax.axis_size("row")
    local_frames, local_tokens, width = spatial_q.shape
    head_size = D // HEADS
    scale = head_size ** (-0.5)
    pool_size = local_tokens * row_count // AGENTS
    own_agents = local_tokens // pool_size
    pooled = jnp.mean(
        spatial_q.reshape(local_frames, own_agents, pool_size, width), axis=2, dtype=jnp.float32
    )
    agents = gather_directly(pooled.astype(jnp.bfloat16), "row", 1)
    agent_heads = agents.reshape(local_frames, AGENTS, HEADS, head_size)
    query_heads = spatial_q.reshape(local_frames, local_tokens, HEADS, head_size)
    key_heads = spatial_k.reshape(local_frames, local_tokens, HEADS, head_size)
    value_heads = spatial_v.reshape(local_frames, local_tokens, HEADS, head_size)
    agent_scores = (
        jnp.einsum("fahd,fthd->fhat", agent_heads, key_heads, preferred_element_type=jnp.float32)
        * scale
    )
    peak = taken_together(jnp.max(agent_scores, axis=-1), "row")
    agent_weights = jnp.exp(agent_scores - peak[..., None])
    agent_totals = jnp.sum(agent_weights, axis=-1)
    agent_numer = jnp.einsum(
        "fhat,fthd->fhad",
        agent_weights.astype(jnp.bfloat16),
        value_heads,
        preferred_element_type=jnp.float32,
    )
    owned_totals, owned_numer = in_one_piece((agent_totals, agent_numer), "row", 2, 3)
    owned_values = (owned_numer / owned_totals[..., None]).astype(jnp.bfloat16)
    agent_values = gather_directly(owned_values, "row", 2)
    token_scores = (
        jnp.einsum("fthd,fahd->fhta", query_heads, agent_heads, preferred_element_type=jnp.float32)
        * scale
    )
    token_weights = jax.nn.softmax(token_scores, axis=-1).astype(jnp.bfloat16)
    spatial_out = jnp.einsum(
        "fhta,fhad->fthd", token_weights, agent_values, preferred_element_type=jnp.float32
    )
    spatial_out = spatial_out.reshape(local_frames, local_tokens, width)
    mean_square = jnp.mean(spatial_out * spatial_out, axis=-1, keepdims=True)
    normed = (spatial_out * lax.rsqrt(mean_square + epsilon) * norm_gain).astype(jnp.bfloat16)
    slot_size = local_tokens // frame_count
    group_width = temporal_weight.shape[2]
    group_heads = group_width // head_size
    all_frames = local_frames * frame_count
    locations = row_count * slot_size
    packed = normed.reshape(local_frames, frame_count, slot_size, width)
    moved = lax.all_to_all(packed, "frame", split_axis=1, concat_axis=0, tiled=True)
    moved = moved.reshape(all_frames, slot_size, width)
    projected = jnp.einsum(
        "ftd,dcn->ftcn",
        lax.all_gather(moved, "row", axis=1, tiled=True),
        temporal_weight,
        preferred_element_type=jnp.float32,
    )
    qkv = projected.astype(jnp.bfloat16).reshape(all_frames, locations, 3, group_heads, head_size)
    temporal_scores = (
        jnp.einsum(
            "flhd,glhd->lhfg", qkv[:, :, 0], qkv[:, :, 1], preferred_element_type=jnp.float32
        )
        * scale
    )
    temporal_weights = jax.nn.softmax(temporal_scores, axis=-1).astype(jnp.bfloat16)
    attended = jnp.einsum(
        "lhfg,glhd->flhd", temporal_weights, qkv[:, :, 2], preferred_element_type=jnp.float32
    )
    attended = attended.astype(jnp.bfloat16).reshape(
        all_frames, row_count, 1, slot_size, group_width
    )
    frame_home = lax.all_to_all(attended, "frame", split_axis=0, concat_axis=2, tiled=True)
    returned = lax.all_to_all(frame_home, "row", split_axis=1, concat_axis=4, tiled=True)
    return returned.reshape(local_frames, local_tokens, width)


def solution(mesh):
    return jax.shard_map(
        local,
        mesh=mesh,
        in_specs=(
            P("frame", "row", None),
            P("frame", "row", None),
            P("frame", "row", None),
            P(),
            P(None, None, "row"),
        ),
        out_specs=P("frame", "row", None),
        check_vma=False,
    )
```

profile of v0, /device:TPU:194, one launch (start us, length us, event | category | flops | bytes accessed | tf_op | source)
XLA Modules:
  0.0 419.1 jit_solution(6250770703293055484)
XLA Ops:
  6.5 1.6 convert_reduce_fusion
  9.2 9.6 %all-to-all-start = ((bf16[8,1,16,3072]{3,2,1,0:T(8,128)(2,1)}), bf16[8,1,16,3072]{3,2,1,0:T(8,128)(2,1)S(1)}, u32[]{:S(2)}, u32[]{:S(2)}) async-start(bf16[8,1,16,3072]{3,2,1,0:T(8,128)(2,1)} %broadcast_in_dim.8), calls=%async_computation | async-start | bytes 1572864 | tf_op jit(solution)/shard_map/all_to_all | solution.py:22
  19.0 18.1 %all-to-all-done = bf16[8,1,16,3072]{3,2,1,0:T(8,128)(2,1)S(1)} async-done(((bf16[8,1,16,3072]{3,2,1,0:T(8,128)(2,1)}), bf16[8,1,16,3072]{3,2,1,0:T(8,128)(2,1)S(1)}, u32[]{:S(2)}, u32[]{:S(2)}) %all-to-all-start) | async-done | bytes 786464 | tf_op jit(solution)/shard_map/all_to_all | solution.py:22
  38.7 10.3 %all-to-all-start.1 = ((f32[8,1,24,128]{3,2,1,0:T(8,128)}), f32[8,1,24,128]{3,2,1,0:T(8,128)S(1)}, u32[]{:S(2)}, u32[]{:S(2)}) async-start(f32[8,1,24,128]{3,2,1,0:T(8,128)} %broadcast_in_dim.9), calls=%async_computation.1 | async-start | bytes 196608 | tf_op jit(solution)/shard_map/all_to_all | solution.py:22
  49.0 1.0 copy.144
  50.0 3.3 all-to-all-done.1
  55.1 1.2 copy.106
  57.2 69.5 %all_to_all.62 = f32[8,1,24,16,129]{4,3,2,1,0:T(8,128)S(1)} all-to-all(f32[8,1,24,16,129]{4,3,2,1,0:T(8,128)S(1)} %maximum_bitcast_fusion), channel_id=1, replica_groups=mesh['frame'=32,'row'=8] {'row'}, dimensions={0} | all-to-all | bytes 3170304 | tf_op jit(solution)/shard_map/all_to_all | solution.py:41
  127.5 1.0 broadcast_in_dim.11
  128.5 10.2 %all-to-all-start.3 = ((bf16[8,1,24,16,128]{4,3,2,1,0:T(8,128)(2,1)}), bf16[8,1,24,16,128]{4,3,2,1,0:T(8,128)(2,1)S(1)}, u32[]{:S(2)}, u32[]{:S(2)}) async-start(bf16[8,1,24,16,128]{4,3,2,1,0:T(8,128)(2,1)} %broadcast_in_dim.11), calls=%async_computation.3 | async-start | bytes 1572864 | tf_op jit(solution)/shard_map/all_to_all | solution.py:22
  138.9 1.3 fusion.53
  140.1 1.8 convolution_multiply_fusion.1
  142.0 8.8 %all-to-all-done.3 = bf16[8,1,24,16,128]{4,3,2,1,0:T(8,128)(2,1)S(1)} async-done(((bf16[8,1,24,16,128]{4,3,2,1,0:T(8,128)(2,1)}), bf16[8,1,24,16,128]{4,3,2,1,0:T(8,128)(2,1)S(1)}, u32[]{:S(2)}, u32[]{:S(2)}) %all-to-all-start.3) | async-done | bytes 786464 | tf_op jit(solution)/shard_map/all_to_all | solution.py:22
  151.0 7.2 %multiply_reduce_fusion = (f32[128]{0:T(128)S(1)}, f32[1,128,24,128]{1,3,2,0:T(8,128)S(1)}) fusion(bf16[24,128,128]{2,1,0:T(8,128)(2,1)S(1)} %bitcast.114, f32[24,128]{1,0:T(8,128)S(1)} %fusion.53, f32[24,128,128]{1,2,0:T(8,128)} %convolution_multiply_fusion.1), kind=kOutput, calls=%fused_computation.17 | convolution fusion | flops 102632448 | bytes 3944960 | tf_op jit(solution)/shard_map/fhta,fhad->fthd/dot_general | solution.py:93
  160.6 27.1 %all_to_all.63 = bf16[1,32,4,3072]{3,2,0,1:T(4,128)(2,1)S(1)} all-to-all(bf16[1,32,4,3072]{3,2,0,1:T(4,128)(2,1)S(1)} %copy.119), channel_id=1, replica_groups=mesh['frame'=32,'row'=8] {'frame'}, dimensions={1} | all-to-all | bytes 1572864 | tf_op jit(solution)/shard_map/all_to_all | solution.py:105
  187.8 1.1 copy.120
  188.9 135.5 %all-gather.3.cloned.1.call-done = bf16[1,32,32,3072]{3,1,0,2:T(8,128)(2,1)} async-done(((bf16[1,32,4,3072]{3,1,0,2:T(8,128)(2,1)}), bf16[1,32,32,3072]{3,1,0,2:T(8,128)(2,1)}) %all-gather.3.cloned.1.call-update) | async-done | bytes 6291472 | tf_op jit(solution)/shard_map/all_gather | solution.py:109
  324.4 16.8 %fusion.6 = bf16[32,32,3,384]{3,1,2,0:T(8,128)(2,1)} fusion(bf16[3072,3,384]{2,0,1:T(8,128)(2,1)} %param.9, bf16[1,32,32,3072]{3,1,0,2:T(8,128)(2,1)} %all-gather.3.cloned.1.call-done), kind=kOutput, calls=%fused_computation.7 | convolution fusion | flops 7248936960 | bytes 15728640 | tf_op jit(solution)/shard_map/ftd,dcn->ftcn/dot_general | solution.py:107
  341.2 5.9 %reshape.197 = bf16[32,32,3,3,128]{4,3,1,2,0:T(4,128)(2,1)S(1)} reshape(bf16[32,32,3,384]{3,1,2,0:T(8,128)(2,1)} %fusion.6) | data formatting | bytes 4718592 | tf_op jit(solution)/shard_map/reshape | solution.py:113
  347.1 2.7 fusion.51
  349.8 3.3 fusion.60
  355.2 26.9 %all_to_all.64 = bf16[32,8,1,4,384]{4,3,1,2,0:T(4,128)(2,1)S(1)} all-to-all(bf16[32,8,1,4,384]{4,3,1,2,0:T(4,128)(2,1)S(1)} %reshape.204), channel_id=1, replica_groups=mesh['frame'=32,'row'=8] {'frame'}, dimensions={0} | all-to-all | bytes 1572864 | tf_op jit(solution)/shard_map/all_to_all | solution.py:127
  382.4 28.1 %all_to_all.65 = bf16[1,8,32,4,384]{4,2,3,0,1:T(8,128)(2,1)S(1)} all-to-all(bf16[1,8,32,4,384]{4,2,3,0,1:T(8,128)(2,1)S(1)} %copy.128), channel_id=1, replica_groups=mesh['frame'=32,'row'=8] {'row'}, dimensions={1} | all-to-all | bytes 1572864 | tf_op jit(solution)/shard_map/all_to_all | solution.py:128
  411.0 1.2 reshape.199
  (46 shorter events, 11.7 us)
Async XLA Ops:
  8.2 10.6 %copy-start.5 = (bf16[1,128,3072]{2,1,0:T(8,128)(2,1)S(1)}, bf16[1,128,3072]{2,1,0:T(8,128)(2,1)}, u32[]{:S(2)}) copy-start(bf16[1,128,3072]{2,1,0:T(8,128)(2,1)} %param.6) | copy-start | bytes 2359300
  9.2 27.9 %all-to-all-start = ((bf16[8,1,16,3072]{3,2,1,0:T(8,128)(2,1)}), bf16[8,1,16,3072]{3,2,1,0:T(8,128)(2,1)S(1)}, u32[]{:S(2)}, u32[]{:S(2)}) async-start(bf16[8,1,16,3072]{3,2,1,0:T(8,128)(2,1)} %broadcast_in_dim.8), calls=%async_computation | async-start | bytes 1572864 | tf_op jit(solution)/shard_map/all_to_all | solution.py:22
  37.2 0.9 copy-start
  37.2 11.8 %copy-start.6 = (bf16[1,128,3072]{2,1,0:T(8,128)(2,1)S(1)}, bf16[1,128,3072]{2,1,0:T(8,128)(2,1)}, u32[]{:S(2)}) copy-start(bf16[1,128,3072]{2,1,0:T(8,128)(2,1)} %param.7) | copy-start | bytes 2359300
  38.7 14.6 %all-to-all-start.1 = ((f32[8,1,24,128]{3,2,1,0:T(8,128)}), f32[8,1,24,128]{3,2,1,0:T(8,128)S(1)}, u32[]{:S(2)}, u32[]{:S(2)}) async-start(f32[8,1,24,128]{3,2,1,0:T(8,128)} %broadcast_in_dim.9), calls=%async_computation.1 | async-start | bytes 196608 | tf_op jit(solution)/shard_map/all_to_all | solution.py:22
  53.4 1.1 copy-start.3
  127.1 11.6 %copy-start.2 = (bf16[1,128,3072]{2,1,0:T(8,128)(2,1)S(1)}, bf16[1,128,3072]{2,1,0:T(8,128)(2,1)}, u32[]{:S(2)}) copy-start(bf16[1,128,3072]{2,1,0:T(8,128)(2,1)} %param.5) | copy-start | bytes 2359300
  128.5 10.4 %copy-start.1 = (bf16[16,8,24,128]{3,2,1,0:T(8,128)(2,1)S(1)}, bf16[16,8,24,128]{3,2,1,0:T(8,128)(2,1)}, u32[]{:S(2)}) copy-start(bf16[16,8,24,128]{3,2,1,0:T(8,128)(2,1)} %copy-done) | copy-start | bytes 2359300
  128.5 22.3 %all-to-all-start.3 = ((bf16[8,1,24,16,128]{4,3,2,1,0:T(8,128)(2,1)}), bf16[8,1,24,16,128]{4,3,2,1,0:T(8,128)(2,1)S(1)}, u32[]{:S(2)}, u32[]{:S(2)}) async-start(bf16[8,1,24,16,128]{4,3,2,1,0:T(8,128)(2,1)} %broadcast_in_dim.11), calls=%async_computation.3 | async-start | bytes 1572864 | tf_op jit(solution)/shard_map/all_to_all | solution.py:22
  138.7 185.7 %all-gather.3.cloned.1.call-start = ((), (), s32[]{:S(2)}) async-start(), calls=%async_computation.7 | async-start | bytes 7077888 | tf_op jit(solution)/shard_map/all_gather | solution.py:109
  158.4 0.7 copy-start.7
  349.8 3.3 copy-start.4
Sparse Core Ops, SparseCore 0:
  189.0 135.3 all-gather.2
where the time goes:
time: 427 us; the launch traced here: 419 us
  waiting for transfers between devices  166 us (39%)
  blocking collectives  152 us (36%)
  matrix products  32.4 us (8%)
  starting transfers between devices  30.1 us (7%)
  local copies, waits for them, and re-layouts  21.2 us (5%)
  between operations  13.6 us (3%)
  other arithmetic  4.28 us (1%)
    all_gather x1, waiting for transfers between devices, local(): lax.all_gather(moved, 'row', axis=1, tiled=True)  136 us
    all_to_all x1, blocking collectives, sent_and_summed(): lax.all_to_all(tiles, axis, split_axis=0, concat_axis=0, tiled=True)  69.5 us
    all_to_all x3, waiting for transfers between devices, from_everyone(): lax.all_to_all(jnp.broadcast_to(x[None], (size, *x.shape)), axis, 0, 0, t...  30.2 us
    all_to_all x3, starting transfers between devices, from_everyone(): lax.all_to_all(jnp.broadcast_to(x[None], (size, *x.shape)), axis, 0, 0, t...  30.1 us
    all_to_all x1, blocking collectives, local(): lax.all_to_all(frame_home, 'row', split_axis=1, concat_axis=4, tiled=True)  28.1 us
    all_to_all x1, blocking collectives, local(): lax.all_to_all(packed, 'frame', split_axis=1, concat_axis=0, tiled=True)  27.1 us
    all_to_all x1, blocking collectives, local(): lax.all_to_all(attended, 'frame', split_axis=0, concat_axis=2, tiled=True)  26.9 us
    dot_general x1, matrix products, local(): jnp.einsum('ftd,dcn->ftcn', lax.all_gather(moved, 'row', axis=1, tiled=Tr...  16.8 us
  transfers between devices with their start and end apart: 4, of which 4 were waited for; matrix products, arithmetic and copies ran while one was open for 1% of the time, Pallas kernels for 0%

commit v1 on v0

v1 whole, which is shorter than its diff:
```python
import jax
import jax.numpy as jnp
from jax import lax
from jax.experimental import pallas as pl
from jax.experimental.pallas import tpu as pltpu
from jax.sharding import PartitionSpec as P

D = 3072
HEAD = 128
TOK = 128
XCOLS = D // 4
XHEADS = XCOLS // HEAD
HALF_TOK = 4 * TOK
LOC = 16
NCOLS = D // 8
NHEADS = NCOLS // HEAD
SCALE = HEAD ** (-0.5)
EPS = 1e-06
F32 = jnp.float32
BF16 = jnp.bfloat16
MESH = pl.DeviceIdType.MESH


def aligned(i, n):
    return pl.multiple_of(i * n, n)


def kernel(
    q_hbm, k_hbm, v_hbm, gain, w_hbm, out,
    qx, kx, vx, ag, tw, pb, nb, st, sb, wv, ws, xb, acc, ssq, of, ob, rb,
    a_send, a_recv, a_loc, z_send, z_recv, w_loc, w1_send, w1_recv, w2_send, w2_recv,
    b_send, b_recv, b_loc, x_send, x_recv, s_send, s_recv, c_send, c_recv, c_loc, o_send, o_recv, o_loc,
):
    f = lax.axis_index("frame")
    r = lax.axis_index("row")
    zl, y, c = f // 8, (f // 2) % 4, f % 2
    x, zh = r // 2, r % 2

    def dev(zl_, y_, c_, x_, zh_):
        return ((zl_ * 4 + y_) * 2 + c_, x_ * 2 + zh_)

    def remote(src, dst, ss, rs, to):
        return pltpu.make_async_remote_copy(src, dst, ss, rs, device_id=to, device_id_type=MESH)

    z_dev = dev(zl, y, c, x, 1 - zh)
    sib = dev(zl, y, 1 - c, x, zh)
    owner = c == zh

    def a_copy(t, dx):
        src, dst = ((q_hbm, qx), (k_hbm, kx), (v_hbm, vx))[t]
        xp = (x + dx) % 4
        return remote(
            src.at[:, pl.ds(aligned(xp, XCOLS), XCOLS)],
            dst.at[pl.ds(aligned(x, TOK), TOK), :],
            a_send.at[t, dx], a_recv.at[t, dx], dev(zl, y, c, xp, zh),
        )

    def a_local(t):
        src, dst = ((q_hbm, qx), (k_hbm, kx), (v_hbm, vx))[t]
        return pltpu.make_async_copy(
            src.at[:, pl.ds(aligned(x, XCOLS), XCOLS)], dst.at[pl.ds(aligned(x, TOK), TOK), :], a_loc.at[t]
        )

    def a_wait(t):
        for dx in (1, 3, 2):
            a_copy(t, dx).wait_recv()
        a_local(t).wait()

    for t in range(3):
        for dx in (1, 3, 2):
            a_copy(t, dx).start()
        a_local(t).start()

    rows_y = pl.ds(aligned(y, 768), 768)

    def w1_copy(i):
        return remote(w_hbm.at[i, rows_y, :], wv.at[i, rows_y, :], w1_send.at[i], w1_recv.at[i], z_dev)

    def w_local():
        return pltpu.make_async_copy(w_hbm, wv, w_loc)

    def w2_copy(i, dy):
        to = dev(zl, (y + dy) % 4, c, x, zh)
        return remote(wv.at[i, rows_y, :], wv.at[i, rows_y, :], w2_send.at[i, dy], w2_recv.at[i, dy], to)

    @pl.when(owner)
    def _():
        for i in range(3):
            w1_copy(i).start()
        w_local().start()

    def w_forward(i):
        @pl.when(jnp.logical_not(owner))
        def _():
            w1_copy(i).wait_recv()
            for dy in (1, 3, 2):
                w2_copy(i, dy).start()

    a_wait(0)
    pool = (
        lax.broadcasted_iota(jnp.int32, (64, HALF_TOK), 1) // 8 == lax.broadcasted_iota(jnp.int32, (64, HALF_TOK), 0)
    ).astype(F32) * 0.125
    ag[zh] = jnp.dot(pool.astype(BF16), qx[...], preferred_element_type=F32).astype(BF16)
    ag_copy = remote(ag.at[zh], ag.at[zh], z_send.at[0], z_recv.at[0], z_dev)
    ag_copy.start()
    ag_copy.wait_recv()

    def nt(a, b):
        return lax.dot_general(a, b, (((1,), (1,)), ((), ())), preferred_element_type=F32)

    def head(h):
        return slice(h * HEAD, (h + 1) * HEAD)

    def agents(h):
        return ag[:, :, head(h)].reshape(2 * 64, HEAD)

    for h in range(XHEADS):
        s = nt(qx[:, head(h)], agents(h)) * SCALE
        e = jnp.exp(s - jnp.max(s, axis=1, keepdims=True))
        tw[h] = e * (1.0 / jnp.sum(e, axis=1, keepdims=True))
    w_forward(0)

    a_wait(1)
    lane = lax.broadcasted_iota(jnp.int32, (128, 128), 1)
    stats = jnp.where(lane < 8, 0.0, 1.0)
    for h in range(XHEADS):
        s = nt(agents(h), kx[:, head(h)]) * SCALE
        m = jnp.max(s, axis=1, keepdims=True)
        e = jnp.exp(s - m)
        pb[h] = e.astype(BF16)
        stats = jnp.where(lane == h, m, stats)
        stats = jnp.where(lane == 8 + h, jnp.sum(e, axis=1, keepdims=True), stats)
    st[zh] = stats.T[0:16, :]
    st_copy = remote(st.at[zh], st.at[zh], z_send.at[1], z_recv.at[1], z_dev)
    st_copy.start()
    w_forward(1)
    a_wait(2)
    for h in range(XHEADS):
        nb[zh, h] = jnp.dot(pb[h], vx[:, head(h)], preferred_element_type=F32).astype(BF16)
    nb_copy = remote(nb.at[zh], nb.at[zh], z_send.at[2], z_recv.at[2], z_dev)
    nb_copy.start()
    st_copy.wait_recv()
    m0, m1 = st[0, 0:8, :], st[1, 0:8, :]
    l0, l1 = st[0, 8:16, :], st[1, 8:16, :]
    peak = jnp.maximum(m0, m1)
    e0, e1 = jnp.exp(m0 - peak), jnp.exp(m1 - peak)
    inv = 1.0 / (l0 * e0 + l1 * e1)
    s0, s1 = e0 * inv, e1 * inv
    nb_copy.wait_recv()

    for h in range(XHEADS):
        t = tw[h]
        both = jnp.concatenate([(t * s0[h : h + 1, :]).astype(BF16), (t * s1[h : h + 1, :]).astype(BF16)], axis=1)
        sb[:, head(h)] = jnp.dot(
            both, nb[:, h].reshape(256, HEAD), preferred_element_type=F32
        ).astype(BF16)

    me = (zl * 4 + y) * 2 + zh

    def b_copy(d):
        zl_, y_, zh_ = (zl + d // 8) % 4, (y + (d // 2) % 4) % 4, (zh + d % 2) % 2
        g = y_ * 8 + zh_ * 4 + zl_
        return remote(
            sb.at[pl.ds(aligned(g, LOC), LOC), :],
            xb.at[c, x, pl.ds(aligned(me, LOC), LOC), :],
            b_send.at[d], b_recv.at[d], dev(zl_, y_, c, x, zh_),
        )

    def b_wait(d):
        zl_, y_, zh_ = (zl + 4 - d // 8) % 4, (y + 4 - (d // 2) % 4) % 4, (zh + d % 2) % 2
        row = (zl_ * 4 + y_) * 2 + zh_
        dst = xb.at[c, x, pl.ds(aligned(row, LOC), LOC), :]
        remote(dst, dst, b_send.at[d], b_recv.at[d], z_dev).wait_recv()

    group = y * 8 + zh * 4 + zl
    own = pltpu.make_async_copy(
        sb.at[pl.ds(aligned(group, LOC), LOC), :], xb.at[c, x, pl.ds(aligned(me, LOC), LOC), :], b_loc
    )
    own.start()

    @pl.loop(1, 32)
    def _(d):
        b_copy(d).start()

    w_forward(2)

    @pl.when(owner)
    def _():
        w_local().wait()

    @pl.when(jnp.logical_not(owner))
    def _():
        for i in range(3):
            for dy in (1, 3, 2):
                dst = wv.at[i, pl.ds(aligned((y + 4 - dy) % 4, 768), 768), :]
                remote(dst, dst, w2_send.at[i, dy], w2_recv.at[i, dy], z_dev).wait_recv()
            for dy in (1, 3, 2):
                w2_copy(i, dy).wait_send()

    @pl.loop(0, D // 128)
    def _(kc):
        g = jnp.broadcast_to(gain[pl.ds(kc, 1), :], (128, 128)).T
        rows = pl.ds(aligned(kc, 128), 128)
        for i in range(3):
            for j in range(NHEADS):
                piece = wv[i, rows, head(j)].astype(F32) * g
                ws[rows, i * NCOLS + j * HEAD : i * NCOLS + (j + 1) * HEAD] = piece.astype(BF16)

    left, right, far = (x + 3) % 4, (x + 1) % 4, (x + 2) % 4

    def block(half, col, s, lo=0, n=128):
        zl_ = (zl + 4 - s) % 4
        return xb.at[half, col, pl.ds(pl.multiple_of(zl_ * 128 + lo, 64), n), :]

    def x_own(s, i):
        b = block(c, x, s)
        return remote(b, b, x_send.at[s, i], x_recv.at[s, i], dev(zl, y, c, (right, left)[i], zh))

    def x_fwd(s, i):
        b = block(c, (left, right)[i], s, 64 * i, 64)
        return remote(b, b, x_send.at[s, 2 + i], x_recv.at[s, 2 + i], dev(zl, y, c, (right, left)[i], zh))

    def x_got(s, i):
        col = (left, right, far, far)[i]
        b = block(c, col, s, *((0, 128), (0, 128), (0, 64), (64, 64))[i])
        return remote(b, b, x_send.at[s, i], x_recv.at[s, i], z_dev)

    def to_sib(s, i):
        b = block(c, (x, left, right, far)[i], s)
        return remote(b, b, s_send.at[s, i], s_recv.at[s, i], sib)

    def from_sib(s, i):
        b = block(1 - c, (x, left, right, far)[i], s)
        return remote(b, b, s_send.at[s, i], s_recv.at[s, i], sib)

    def mm(half, col, first=False):
        rows_w = pl.ds(aligned(col, XCOLS), XCOLS)

        @pl.loop(0, 2)
        def _(i):
            src = xb[half, col, pl.ds(aligned(i, 256), 256), :]
            rows = pl.ds(pl.multiple_of(half * 512 + i * 256, 256), 256)
            p = jnp.dot(src, ws[rows_w, :], preferred_element_type=F32)
            wide = src.astype(F32)
            sq = jnp.broadcast_to(jnp.sum(wide * wide, axis=1, keepdims=True), (256, 128))
            for j in range(3 * NHEADS):
                if first:
                    acc[j, rows, :] = p[:, head(j)]
                else:
                    acc[j, rows, :] += p[:, head(j)]
            if first:
                ssq[rows, :] = sq
            else:
                ssq[rows, :] += sq

    for s in range(6):
        if s < 4:
            if s == 0:
                own.wait()
            for d in range(8 * s, 8 * s + 8):
                if d:
                    b_wait(d)
            x_own(s, 0).start()
            x_own(s, 1).start()
            to_sib(s, 0).start()
        if 1 <= s < 5:
            for i in range(2):
                x_got(s - 1, i).wait_recv()
                x_fwd(s - 1, i).start()
                to_sib(s - 1, 1 + i).start()
        if s == 3:
            mm(c, x, True)
        if s == 4:
            for q in range(4):
                from_sib(q, 0).wait_recv()
            mm(1 - c, x, True)
        if s >= 2:
            for i in (2, 3):
                x_got(s - 2, i).wait_recv()
            to_sib(s - 2, 3).start()
        if s == 4:
            mm(c, left)
            mm(c, right)
    for q in range(4):
        from_sib(q, 1).wait_recv()
        from_sib(q, 2).wait_recv()
    mm(1 - c, left)
    mm(1 - c, right)
    mm(c, far)
    for q in range(4):
        from_sib(q, 3).wait_recv()
    mm(1 - c, far)
    ssq[...] = lax.rsqrt(ssq[...] * (1.0 / D) + EPS)

    same = (
        lax.broadcasted_iota(jnp.int32, (128, 128), 0) // 32 == lax.broadcasted_iota(jnp.int32, (128, 128), 1) // 32
    )

    def c_copy(d, h):
        zl_, y_, c_ = (zl + d // 8) % 4, (y + (d // 2) % 4) % 4, (c + d % 2) % 2
        row = c_ * 512 + (zl_ * 4 + y_) * 32 + h * LOC
        hs = (h + 2 - zh) % 2
        return remote(
            ob.at[pl.ds(pl.multiple_of(row, LOC), LOC), :],
            rb.at[pl.ds(aligned(group, LOC), LOC), pl.ds(aligned(c, NCOLS), NCOLS)],
            c_send.at[hs, d], c_recv.at[hs, d], dev(zl_, y_, c_, x, h),
        )

    def c_own():
        row = c * 512 + (zl * 4 + y) * 32 + zh * LOC
        return pltpu.make_async_copy(
            ob.at[pl.ds(pl.multiple_of(row, LOC), LOC), :],
            rb.at[pl.ds(aligned(group, LOC), LOC), pl.ds(aligned(c, NCOLS), NCOLS)], c_loc,
        )

    for part in range(2):

        @pl.loop(part * 4, part * 4 + 4)
        def _(b):
            picks = [pl.ds(b * 4 + i, 32, stride=32) for i in range(4)]
            norm = jnp.concatenate([ssq[p, :] for p in picks], axis=0)

            def rows_of(j):
                return (jnp.concatenate([acc[j, p, :] for p in picks], axis=0) * norm).astype(BF16)

            for h in range(NHEADS):
                s = nt(rows_of(h), rows_of(NHEADS + h)) * SCALE
                s = jnp.where(same, s, -1e30)
                e = jnp.exp(s - jnp.max(s, axis=1, keepdims=True))
                p = (e * (1.0 / jnp.sum(e, axis=1, keepdims=True))).astype(BF16)
                o = jnp.dot(p, rows_of(2 * NHEADS + h), preferred_element_type=F32)
                for i in range(4):
                    of[h, picks[i], :] = o[32 * i : 32 * i + 32, :]

        @pl.loop(0, 32)
        def _(k):
            rows = pl.ds(pl.multiple_of(k * 32 + part * LOC, LOC), LOC)
            for h in range(NHEADS):
                ob[rows, head(h)] = of[h, rows, :].astype(BF16)

        @pl.loop(1, 32)
        def _(d):
            c_copy(d, part).start()

        @pl.when(zh == part)
        def _():
            c_own().start()

        @pl.when(zh != part)
        def _():
            c_copy(0, part).start()

    c_own().wait()

    def c_wait(hs, d):
        zl_, y_, c_ = (zl + 4 - d // 8) % 4, (y + 4 - (d // 2) % 4) % 4, (c + d % 2) % 2
        zh_ = (zh + hs) % 2
        g = y_ * 8 + zh_ * 4 + zl_
        dst = rb.at[pl.ds(aligned(g, LOC), LOC), pl.ds(aligned(c_, NCOLS), NCOLS)]
        remote(dst, dst, c_send.at[hs, d], c_recv.at[hs, d], z_dev).wait_recv()

    @pl.loop(1, 64)
    def _(d):
        c_wait(d // 32, d % 32)

    def o_copy(dx):
        xp = (x + dx) % 4
        return remote(
            rb.at[pl.ds(aligned(xp, TOK), TOK), :], out.at[:, pl.ds(aligned(x, XCOLS), XCOLS)],
            o_send.at[dx], o_recv.at[dx], dev(zl, y, c, xp, zh),
        )

    for dx in (1, 3, 2):
        o_copy(dx).start()
    mine = pltpu.make_async_copy(
        rb.at[pl.ds(aligned(x, TOK), TOK), :], out.at[:, pl.ds(aligned(x, XCOLS), XCOLS)], o_loc
    )
    mine.start()

    for t in range(3):
        for dx in (1, 3, 2):
            a_copy(t, dx).wait_send()

    @pl.when(owner)
    def _():
        for i in range(3):
            w1_copy(i).wait_send()

    ag_copy.wait_send()
    st_copy.wait_send()
    nb_copy.wait_send()

    @pl.loop(1, 32)
    def _(d):
        b_copy(d).wait_send()

    for s in range(4):
        for i in range(2):
            x_own(s, i).wait_send()
            x_fwd(s, i).wait_send()
        for i in range(4):
            to_sib(s, i).wait_send()

    @pl.loop(1, 64)
    def _(d):
        c_copy(d % 32, (zh + d // 32) % 2).wait_send()

    mine.wait()
    for dx in (1, 3, 2):
        o_copy(dx).wait_send()
    for dx in (1, 3, 2):
        dst = out.at[:, pl.ds(aligned((x + 4 - dx) % 4, XCOLS), XCOLS)]
        src = rb.at[pl.ds(0, TOK), :]
        remote(src, dst, o_send.at[dx], o_recv.at[dx], z_dev).wait_recv()


def local(spatial_q, spatial_k, spatial_v, norm_gain, temporal_weight):
    dma = pltpu.SemaphoreType.DMA
    flat = [a.reshape(TOK, D) for a in (spatial_q, spatial_k, spatial_v)]
    hbm = pl.BlockSpec(memory_space=pl.ANY)
    out = pl.pallas_call(
        kernel,
        out_shape=jax.ShapeDtypeStruct((TOK, D), BF16),
        in_specs=[hbm, hbm, hbm, pl.BlockSpec(memory_space=pltpu.VMEM), hbm],
        out_specs=hbm,
        scratch_shapes=[
            pltpu.VMEM((HALF_TOK, XCOLS), BF16),
            pltpu.VMEM((HALF_TOK, XCOLS), BF16),
            pltpu.VMEM((HALF_TOK, XCOLS), BF16),
            pltpu.VMEM((2, 64, XCOLS), BF16),
            pltpu.VMEM((XHEADS, HALF_TOK, 128), F32),
            pltpu.VMEM((XHEADS, 128, HALF_TOK), BF16),
            pltpu.VMEM((2, XHEADS, 128, HEAD), BF16),
            pltpu.VMEM((2, 16, 128), F32),
            pltpu.VMEM((HALF_TOK, XCOLS), BF16),
            pltpu.VMEM((3, D, NCOLS), BF16),
            pltpu.VMEM((D, 3 * NCOLS), BF16),
            pltpu.VMEM((2, 4, HALF_TOK, XCOLS), BF16),
            pltpu.VMEM((3 * NHEADS, 1024, HEAD), F32),
            pltpu.VMEM((1024, 128), F32),
            pltpu.VMEM((NHEADS, 1024, HEAD), F32),
            pltpu.VMEM((1024, NCOLS), BF16),
            pltpu.VMEM((HALF_TOK, XCOLS), BF16),
            dma((3, 4)), dma((3, 4)), dma((3,)),
            dma((3,)), dma((3,)),
            dma, dma((3,)), dma((3,)), dma((3, 4)), dma((3, 4)),
            dma((32,)), dma((32,)), dma,
            dma((4, 4)), dma((4, 4)),
            dma((4, 4)), dma((4, 4)),
            dma((2, 32)), dma((2, 32)), dma,
            dma((4,)), dma((4,)), dma,
        ],
        compiler_params=pltpu.CompilerParams(has_side_effects=True, vmem_limit_bytes=56 << 20),
    )(*flat, norm_gain.reshape(D // 128, 128), temporal_weight.transpose(1, 0, 2))
    return out.reshape(1, TOK, D)


def solution(mesh):
    return jax.shard_map(
        local,
        mesh=mesh,
        in_specs=(
            P("frame", "row", None),
            P("frame", "row", None),
            P("frame", "row", None),
            P(),
            P(None, None, "row"),
        ),
        out_specs=P("frame", "row", None),
        check_vma=False,
    )
```

time: 427 us -> 182 us (0.43); the launches traced: 419 us -> 181 us
  Pallas kernels: 0 us -> 179 us
  waiting for transfers between devices: 166 us -> 0 us
  blocking collectives: 152 us -> 0 us
  matrix products: 32.4 us -> 0 us
  starting transfers between devices: 30.1 us -> 0 us
  local copies, waits for them, and re-layouts: 21.2 us -> 2.06 us
  between operations: 13.6 us -> 0.01 us
  other arithmetic: 4.28 us -> 0 us
    pallas_call x0 -> x1, Pallas kernels: none -> 179 us  [local(): pl.pallas_call(kernel, out_shape=jax.ShapeDtypeStruct((TOK, D), BF16), in...]
    all_to_all x4 -> x0, blocking collectives: 152 us -> none  [the longest x1 69.5 us: sent_and_summed(): lax.all_to_all(tiles, axis, split_axis=0, concat_axis=0, tiled=True)]
    all_gather x1 -> x0, waiting for transfers between devices: 136 us -> none  [local(): lax.all_gather(moved, 'row', axis=1, tiled=True)]
    all_to_all x3 -> x0, waiting for transfers between devices: 30.2 us -> none  [from_everyone(): lax.all_to_all(jnp.broadcast_to(x[None], (size, *x.shape)), axis, 0, 0, t...]
    all_to_all x3 -> x0, starting transfers between devices: 30.1 us -> none  [from_everyone(): lax.all_to_all(jnp.broadcast_to(x[None], (size, *x.shape)), axis, 0, 0, t...]
    dot_general x6 -> x0, matrix products: 27.8 us -> none  [the longest x1 16.8 us: local(): jnp.einsum('ftd,dcn->ftcn', lax.all_gather(moved, 'row', axis=1, tiled=Tr...]
    reshape x4 -> x0, local copies, waits for them, and re-layouts: 8.38 us -> none  [the longest x1 5.89 us: local(): projected.astype(jnp.bfloat16)]
    sub x2 -> x0, matrix products: 4.57 us -> none  [the longest x1 3.32 us: local(): jax.nn.softmax(temporal_scores, axis=-1).astype(jnp.bfloat16)]
  transfers between devices with their start and end apart: 4 -> 0, of which waited for: 4 -> 0; matrix products, arithmetic and copies ran while one was open for 1% -> 0% of each run, Pallas kernels for 0% -> 0%
where the time goes in v1:
time: 182 us; the launch traced here: 181 us
  Pallas kernels  179 us (98%)
  local copies, waits for them, and re-layouts  2.06 us (1%)
    pallas_call x1, Pallas kernels, local(): pl.pallas_call(kernel, out_shape=jax.ShapeDtypeStruct((TOK, D), BF16), in...  179 us

profile of v1, /device:TPU:194, one launch (start us, length us, event | category | flops | bytes accessed | tf_op | source)
XLA Modules:
  0.0 180.8 jit_solution(4896003946171439093)
XLA Ops:
  0.0 178.7 %shard_map.55 = bf16[128,3072]{1,0:T(8,128)(2,1)} custom-call(bf16[128,3072]{1,0:T(8,128)(2,1)} %bitcast.8, bf16[128,3072]{1,0:T(8,128)(2,1)} %bitcast.9, bf16[128,3072]{1,0:T(8,128)(2,1)} %bitcast.10, f32[24,128]{1,0:T(8,128)} %bitcast.11, bf16[3,3072,384]{2,1,0:T(8,128)(2,1)} %bitcast.6), custom_call_target="tpu_custom_call" | custom-call | tf_op jit(solution)/shard_map/pallas_call | solution.py:421
  178.7 2.1 %copy.7 = bf16[1,128,3072]{2,1,0:T(8,128)(2,1)} copy(bf16[1,128,3072]{2,1,0:T(8,128)(2,1)} %bitcast.7) | data formatting | bytes 1572864

commit v2 on v1

--- a/solution.py
+++ b/solution.py
@@ -28,7 +28,7 @@
 def kernel(
     q_hbm, k_hbm, v_hbm, gain, w_hbm, out,
     qx, kx, vx, ag, tw, pb, nb, st, sb, wv, ws, xb, acc, ssq, of, ob, rb,
-    a_send, a_recv, a_loc, z_send, z_recv, w_loc, w1_send, w1_recv, w2_send, w2_recv,
+    a_send, a_recv, a_loc, z_send, z_recv, w_loc, w1_send, w1_recv, wi_send, w2_send, w2_recv,
     b_send, b_recv, b_loc, x_send, x_recv, s_send, s_recv, c_send, c_recv, c_loc, o_send, o_recv, o_loc,
 ):
     f = lax.axis_index("frame")
@@ -46,55 +46,110 @@
     sib = dev(zl, y, 1 - c, x, zh)
     owner = c == zh
 
+    barrier = pltpu.get_barrier_semaphore()
+    for dx in (1, 3, 2):
+        pl.semaphore_signal(barrier, inc=1, device_id=dev(zl, y, c, (x + dx) % 4, zh), device_id_type=MESH)
+
+    @pl.loop(1, 64)
+    def _(d):
+        to = dev((zl + d // 16) % 4, (y + (d // 4) % 4) % 4, (c + d % 2) % 2, x, (zh + (d // 2) % 2) % 2)
+        pl.semaphore_signal(barrier, inc=1, device_id=to, device_id_type=MESH)
+
+    half_cols = XCOLS // 2
+    parts = ((q_hbm, qx, 0, XCOLS), (k_hbm, kx, 0, XCOLS), (v_hbm, vx, 0, half_cols), (v_hbm, vx, half_cols, half_cols))
+
+    def a_from(t, xp):
+        src, _, lo, n = parts[t]
+        return src.at[:, pl.ds(pl.multiple_of(xp * XCOLS + lo, 128), n)]
+
+    def a_to(t):
+        _, dst, lo, n = parts[t]
+        return dst.at[pl.ds(aligned(x, TOK), TOK), pl.ds(lo, n)]
+
     def a_copy(t, dx):
-        src, dst = ((q_hbm, qx), (k_hbm, kx), (v_hbm, vx))[t]
         xp = (x + dx) % 4
-        return remote(
-            src.at[:, pl.ds(aligned(xp, XCOLS), XCOLS)],
-            dst.at[pl.ds(aligned(x, TOK), TOK), :],
-            a_send.at[t, dx], a_recv.at[t, dx], dev(zl, y, c, xp, zh),
-        )
+        return remote(a_from(t, xp), a_to(t), a_send.at[t, dx], a_recv.at[t, dx], dev(zl, y, c, xp, zh))
 
     def a_local(t):
-        src, dst = ((q_hbm, qx), (k_hbm, kx), (v_hbm, vx))[t]
-        return pltpu.make_async_copy(
-            src.at[:, pl.ds(aligned(x, XCOLS), XCOLS)], dst.at[pl.ds(aligned(x, TOK), TOK), :], a_loc.at[t]
-        )
+        return pltpu.make_async_copy(a_from(t, x), a_to(t), a_loc.at[t])
 
     def a_wait(t):
         for dx in (1, 3, 2):
             a_copy(t, dx).wait_recv()
         a_local(t).wait()
 
-    for t in range(3):
+    edge = jnp.logical_or(zl == 0, zl == 3)
+    away = jnp.logical_not(owner)
+
+    def piece(y_, p):
+        return ws.at[pl.ds(pl.multiple_of(y_ * 768 + p * 128, 128), 128), :]
+
+    def w1_copy(p):
+        return remote(piece(y, p), piece(y, p), w1_send.at[p], w1_recv.at[p], dev(3 - zl, y, c, x, 1 - zh))
+
+    def wi_copy(p):
+        to = dev(1 + zl // 3, y, c, x, zh)
+        return remote(piece(y, p), piece(y, p), wi_send.at[p], w1_recv.at[p], to)
+
+    def w2_copy(p, dy):
+        to = dev(zl, (y + dy) % 4, c, x, zh)
+        return remote(piece(y, p), piece(y, p), w2_send.at[p, dy], w2_recv.at[p, dy], to)
+
+    def w_forward(point):
+        def some(first, inner):
+            for p in (first, first + 1):
+                w1_copy(p).wait_recv()
+                if not inner:
+                    wi_copy(p).start()
+                for dy in (1, 3, 2):
+                    w2_copy(p, dy).start()
+
+        if point < 3:
+
+            @pl.when(jnp.logical_and(away, edge))
+            def _():
+                some(2 * point, False)
+
+        if point > 0:
+
+            @pl.when(jnp.logical_and(away, jnp.logical_not(edge)))
+            def _():
+                some(2 * point - 2, True)
+
+    def w_scale(first, last):
+        @pl.loop(first, last)
+        def _(i):
+            kc = (y * 6 + i) % 24
+            g = jnp.broadcast_to(gain[pl.ds(kc, 1), :], (128, 128)).T
+            rows = pl.ds(aligned(kc, 128), 128)
+            for i in range(3):
+                for j in range(NHEADS):
+                    scaled = wv[i, rows, j * HEAD : (j + 1) * HEAD].astype(F32) * g
+                    ws[rows, i * NCOLS + j * HEAD : i * NCOLS + (j + 1) * HEAD] = scaled.astype(BF16)
+
+    for t in range(4):
+        a_local(t).start()
+
+    @pl.when(owner)
+    def _():
+        load = pltpu.make_async_copy(w_hbm, wv, w_loc)
+        load.start()
+        load.wait()
+        w_scale(0, 6)
+
+    pl.semaphore_wait(barrier, 66)
+    for t in range(4):
         for dx in (1, 3, 2):
             a_copy(t, dx).start()
-        a_local(t).start()
-
-    rows_y = pl.ds(aligned(y, 768), 768)
-
-    def w1_copy(i):
-        return remote(w_hbm.at[i, rows_y, :], wv.at[i, rows_y, :], w1_send.at[i], w1_recv.at[i], z_dev)
-
-    def w_local():
-        return pltpu.make_async_copy(w_hbm, wv, w_loc)
-
-    def w2_copy(i, dy):
-        to = dev(zl, (y + dy) % 4, c, x, zh)
-        return remote(wv.at[i, rows_y, :], wv.at[i, rows_y, :], w2_send.at[i, dy], w2_recv.at[i, dy], to)
+
+    @pl.when(jnp.logical_and(owner, edge))
+    def _():
+        for p in range(6):
+            w1_copy(p).start()
 
     @pl.when(owner)
     def _():
-        for i in range(3):
-            w1_copy(i).start()
-        w_local().start()
-
-    def w_forward(i):
-        @pl.when(jnp.logical_not(owner))
-        def _():
-            w1_copy(i).wait_recv()
-            for dy in (1, 3, 2):
-                w2_copy(i, dy).start()
+        w_scale(6, 24)
 
     a_wait(0)
     pool = (
@@ -103,6 +158,7 @@
     ag[zh] = jnp.dot(pool.astype(BF16), qx[...], preferred_element_type=F32).astype(BF16)
     ag_copy = remote(ag.at[zh], ag.at[zh], z_send.at[0], z_recv.at[0], z_dev)
     ag_copy.start()
+    w_forward(0)
     ag_copy.wait_recv()
 
     def nt(a, b):
@@ -118,7 +174,7 @@
         s = nt(qx[:, head(h)], agents(h)) * SCALE
         e = jnp.exp(s - jnp.max(s, axis=1, keepdims=True))
         tw[h] = e * (1.0 / jnp.sum(e, axis=1, keepdims=True))
-    w_forward(0)
+    w_forward(1)
 
     a_wait(1)
     lane = lax.broadcasted_iota(jnp.int32, (128, 128), 1)
@@ -133,12 +189,17 @@
     st[zh] = stats.T[0:16, :]
     st_copy = remote(st.at[zh], st.at[zh], z_send.at[1], z_recv.at[1], z_dev)
     st_copy.start()
-    w_forward(1)
-    a_wait(2)
-    for h in range(XHEADS):
-        nb[zh, h] = jnp.dot(pb[h], vx[:, head(h)], preferred_element_type=F32).astype(BF16)
-    nb_copy = remote(nb.at[zh], nb.at[zh], z_send.at[2], z_recv.at[2], z_dev)
-    nb_copy.start()
+    w_forward(2)
+
+    def nb_copy(i):
+        half = nb.at[zh, 3 * i : 3 * i + 3]
+        return remote(half, half, z_send.at[2 + i], z_recv.at[2 + i], z_dev)
+
+    for i in range(2):
+        a_wait(2 + i)
+        for h in range(3 * i, 3 * i + 3):
+            nb[zh, h] = jnp.dot(pb[h], vx[:, head(h)], preferred_element_type=F32).astype(BF16)
+        nb_copy(i).start()
     st_copy.wait_recv()
     m0, m1 = st[0, 0:8, :], st[1, 0:8, :]
     l0, l1 = st[0, 8:16, :], st[1, 8:16, :]
@@ -146,9 +207,11 @@
     e0, e1 = jnp.exp(m0 - peak), jnp.exp(m1 - peak)
     inv = 1.0 / (l0 * e0 + l1 * e1)
     s0, s1 = e0 * inv, e1 * inv
-    nb_copy.wait_recv()
+    w_forward(3)
 
     for h in range(XHEADS):
+        if h % 3 == 0:
+            nb_copy(h // 3).wait_recv()
         t = tw[h]
         both = jnp.concatenate([(t * s0[h : h + 1, :]).astype(BF16), (t * s1[h : h + 1, :]).astype(BF16)], axis=1)
         sb[:, head(h)] = jnp.dot(
@@ -182,29 +245,12 @@
     def _(d):
         b_copy(d).start()
 
-    w_forward(2)
-
-    @pl.when(owner)
-    def _():
-        w_local().wait()
-
-    @pl.when(jnp.logical_not(owner))
-    def _():
-        for i in range(3):
+    @pl.when(away)
+    def _():
+        for p in range(6):
             for dy in (1, 3, 2):
-                dst = wv.at[i, pl.ds(aligned((y + 4 - dy) % 4, 768), 768), :]
-                remote(dst, dst, w2_send.at[i, dy], w2_recv.at[i, dy], z_dev).wait_recv()
-            for dy in (1, 3, 2):
-                w2_copy(i, dy).wait_send()
-
-    @pl.loop(0, D // 128)
-    def _(kc):
-        g = jnp.broadcast_to(gain[pl.ds(kc, 1), :], (128, 128)).T
-        rows = pl.ds(aligned(kc, 128), 128)
-        for i in range(3):
-            for j in range(NHEADS):
-                piece = wv[i, rows, head(j)].astype(F32) * g
-                ws[rows, i * NCOLS + j * HEAD : i * NCOLS + (j + 1) * HEAD] = piece.astype(BF16)
+                dst = piece((y + 4 - dy) % 4, p)
+                remote(dst, dst, w2_send.at[p, dy], w2_recv.at[p, dy], z_dev).wait_recv()
 
     left, right, far = (x + 3) % 4, (x + 1) % 4, (x + 2) % 4
 
@@ -274,6 +320,12 @@
             for q in range(4):
                 from_sib(q, 0).wait_recv()
             mm(1 - c, x, True)
+        if s == 5:
+            for q in range(4):
+                from_sib(q, 1).wait_recv()
+                from_sib(q, 2).wait_recv()
+            mm(1 - c, left)
+            mm(1 - c, right)
         if s >= 2:
             for i in (2, 3):
                 x_got(s - 2, i).wait_recv()
@@ -281,11 +333,6 @@
         if s == 4:
             mm(c, left)
             mm(c, right)
-    for q in range(4):
-        from_sib(q, 1).wait_recv()
-        from_sib(q, 2).wait_recv()
-    mm(1 - c, left)
-    mm(1 - c, right)
     mm(c, far)
     for q in range(4):
         from_sib(q, 3).wait_recv()
@@ -313,24 +360,27 @@
             rb.at[pl.ds(aligned(group, LOC), LOC), pl.ds(aligned(c, NCOLS), NCOLS)], c_loc,
         )
 
+    def attend(picks):
+        norm = jnp.concatenate([ssq[p, :] for p in picks], axis=0)
+
+        def rows_of(j):
+            return (jnp.concatenate([acc[j, p, :] for p in picks], axis=0) * norm).astype(BF16)
+
+        for h in range(NHEADS):
+            s = nt(rows_of(h), rows_of(NHEADS + h)) * SCALE
+            s = jnp.where(same, s, -1e30)
+            e = jnp.exp(s - jnp.max(s, axis=1, keepdims=True))
+            p = (e * (1.0 / jnp.sum(e, axis=1, keepdims=True))).astype(BF16)
+            o = jnp.dot(p, rows_of(2 * NHEADS + h), preferred_element_type=F32)
+            for i in range(4):
+                of[h, picks[i], :] = o[32 * i : 32 * i + 32, :]
+
     for part in range(2):
 
-        @pl.loop(part * 4, part * 4 + 4)
-        def _(b):
-            picks = [pl.ds(b * 4 + i, 32, stride=32) for i in range(4)]
-            norm = jnp.concatenate([ssq[p, :] for p in picks], axis=0)
-
-            def rows_of(j):
-                return (jnp.concatenate([acc[j, p, :] for p in picks], axis=0) * norm).astype(BF16)
-
-            for h in range(NHEADS):
-                s = nt(rows_of(h), rows_of(NHEADS + h)) * SCALE
-                s = jnp.where(same, s, -1e30)
-                e = jnp.exp(s - jnp.max(s, axis=1, keepdims=True))
-                p = (e * (1.0 / jnp.sum(e, axis=1, keepdims=True))).astype(BF16)
-                o = jnp.dot(p, rows_of(2 * NHEADS + h), preferred_element_type=F32)
-                for i in range(4):
-                    of[h, picks[i], :] = o[32 * i : 32 * i + 32, :]
+        @pl.loop(part * 2, part * 2 + 2)
+        def _(b2):
+            for b in (2 * b2, 2 * b2 + 1):
+                attend([pl.ds(b * 4 + i, 32, stride=32) for i in range(4)])
 
         @pl.loop(0, 32)
         def _(k):
@@ -350,18 +400,22 @@
         def _():
             c_copy(0, part).start()
 
-    c_own().wait()
-
-    def c_wait(hs, d):
-        zl_, y_, c_ = (zl + 4 - d // 8) % 4, (y + 4 - (d // 2) % 4) % 4, (c + d % 2) % 2
-        zh_ = (zh + hs) % 2
-        g = y_ * 8 + zh_ * 4 + zl_
-        dst = rb.at[pl.ds(aligned(g, LOC), LOC), pl.ds(aligned(c_, NCOLS), NCOLS)]
-        remote(dst, dst, c_send.at[hs, d], c_recv.at[hs, d], z_dev).wait_recv()
-
-    @pl.loop(1, 64)
-    def _(d):
-        c_wait(d // 32, d % 32)
+    def c_wait(xs):
+        @pl.loop(0, 16)
+        def _(i):
+            dz, hs, dc = i // 4, (i // 2) % 2, i % 2
+            dy = (y + 4 - xs) % 4
+            d = dz * 8 + dy * 2 + dc
+            g = xs * 8 + ((zh + hs) % 2) * 4 + (zl + 4 - dz) % 4
+            dst = rb.at[pl.ds(aligned(g, LOC), LOC), pl.ds(aligned((c + dc) % 2, NCOLS), NCOLS)]
+
+            @pl.when(d + hs > 0)
+            def _():
+                remote(dst, dst, c_send.at[hs, d], c_recv.at[hs, d], z_dev).wait_recv()
+
+            @pl.when(d + hs == 0)
+            def _():
+                c_own().wait()
 
     def o_copy(dx):
         xp = (x + dx) % 4
@@ -371,24 +425,38 @@
         )
 
     for dx in (1, 3, 2):
+        c_wait((x + dx) % 4)
         o_copy(dx).start()
+    c_wait(x)
     mine = pltpu.make_async_copy(
         rb.at[pl.ds(aligned(x, TOK), TOK), :], out.at[:, pl.ds(aligned(x, XCOLS), XCOLS)], o_loc
     )
     mine.start()
 
-    for t in range(3):
+    for t in range(4):
         for dx in (1, 3, 2):
             a_copy(t, dx).wait_send()
 
-    @pl.when(owner)
-    def _():
-        for i in range(3):
-            w1_copy(i).wait_send()
+    @pl.when(jnp.logical_and(owner, edge))
+    def _():
+        for p in range(6):
+            w1_copy(p).wait_send()
+
+    @pl.when(jnp.logical_and(away, edge))
+    def _():
+        for p in range(6):
+            wi_copy(p).wait_send()
+
+    @pl.when(away)
+    def _():
+        for p in range(6):
+            for dy in (1, 3, 2):
+                w2_copy(p, dy).wait_send()
 
     ag_copy.wait_send()
     st_copy.wait_send()
-    nb_copy.wait_send()
+    for i in range(2):
+        nb_copy(i).wait_send()
 
     @pl.loop(1, 32)
     def _(d):
@@ -441,16 +509,16 @@
             pltpu.VMEM((NHEADS, 1024, HEAD), F32),
             pltpu.VMEM((1024, NCOLS), BF16),
             pltpu.VMEM((HALF_TOK, XCOLS), BF16),
-            dma((3, 4)), dma((3, 4)), dma((3,)),
-            dma((3,)), dma((3,)),
-            dma, dma((3,)), dma((3,)), dma((3, 4)), dma((3, 4)),
+            dma((4, 4)), dma((4, 4)), dma((4,)),
+            dma((4,)), dma((4,)),
+            dma, dma((6,)), dma((6,)), dma((6,)), dma((6, 4)), dma((6, 4)),
             dma((32,)), dma((32,)), dma,
             dma((4, 4)), dma((4, 4)),
             dma((4, 4)), dma((4, 4)),
             dma((2, 32)), dma((2, 32)), dma,
             dma((4,)), dma((4,)), dma,
         ],
-        compiler_params=pltpu.CompilerParams(has_side_effects=True, vmem_limit_bytes=56 << 20),
+        compiler_params=pltpu.CompilerParams(collective_id=0, has_side_effects=True, vmem_limit_bytes=56 << 20),
     )(*flat, norm_gain.reshape(D // 128, 128), temporal_weight.transpose(1, 0, 2))
     return out.reshape(1, TOK, D)
 

time: 182 us -> 148 us (0.81)
  Pallas kernels: 179 us -> 146 us
    pallas_call x1, Pallas kernels: 179 us -> 146 us  [local(): pl.pallas_call(kernel, out_shape=jax.ShapeDtypeStruct((TOK, D), BF16), in...]
where the time goes in v2:
time: 148 us
  Pallas kernels  146 us (99%)
  local copies, waits for them, and re-layouts  2.06 us (1%)
    pallas_call x1, Pallas kernels, local(): pl.pallas_call(kernel, out_shape=jax.ShapeDtypeStruct((TOK, D), BF16), in...  146 us

profile of v2, /device:TPU:194, one launch (start us, length us, event | category | flops | bytes accessed | tf_op | source)
XLA Modules:
  0.0 148.1 jit_solution(7972152691826848235)
XLA Ops:
  0.0 146.1 %shard_map.55 = bf16[128,3072]{1,0:T(8,128)(2,1)} custom-call(bf16[128,3072]{1,0:T(8,128)(2,1)} %bitcast.8, bf16[128,3072]{1,0:T(8,128)(2,1)} %bitcast.9, bf16[128,3072]{1,0:T(8,128)(2,1)} %bitcast.10, f32[24,128]{1,0:T(8,128)} %bitcast.11, bf16[3,3072,384]{2,1,0:T(8,128)(2,1)} %bitcast.6), custom_call_target="tpu_custom_call" | custom-call | tf_op jit(solution)/shard_map/pallas_call | solution.py:489
  146.1 2.1 %copy.7 = bf16[1,128,3072]{2,1,0:T(8,128)(2,1)} copy(bf16[1,128,3072]{2,1,0:T(8,128)(2,1)} %bitcast.7) | data formatting | bytes 1572864

commit v3 on v2

v3 whole, which is shorter than its diff:
```python
import jax
import jax.numpy as jnp
from jax import lax
from jax.experimental import pallas as pl
from jax.experimental.pallas import tpu as pltpu
from jax.sharding import PartitionSpec as P

D = 3072
HEAD = 128
TOK = 128
XCOLS = D // 4
XHEADS = XCOLS // HEAD
HALF_TOK = 4 * TOK
LOC = 16
NCOLS = D // 8
NHEADS = NCOLS // HEAD
SCALE = HEAD ** (-0.5)
EPS = 1e-06
F32 = jnp.float32
BF16 = jnp.bfloat16
MESH = pl.DeviceIdType.MESH


def aligned(i, n):
    return pl.multiple_of(i * n, n)


def kernel(
    q_hbm, k_hbm, v_hbm, gain, w_hbm, out,
    qx, kx, vx, ag, tw, pb, nb, st, sb, wv, ws, xb, acc, ssq, ob, rb,
    a_send, a_recv, a_loc, z_send, z_recv, w_loc, w1_send, w1_recv, wi_send, w2_send, w2_recv,
    b_send, b_recv, b_loc, x_send, x_recv, s_send, s_recv, c_send, c_recv, c_loc, o_send, o_recv, o_loc,
):
    f = lax.axis_index("frame")
    r = lax.axis_index("row")
    zl, y, c = f // 8, (f // 2) % 4, f % 2
    x, zh = r // 2, r % 2

    def dev(zl_, y_, c_, x_, zh_):
        return ((zl_ * 4 + y_) * 2 + c_, x_ * 2 + zh_)

    def remote(src, dst, ss, rs, to):
        return pltpu.make_async_remote_copy(src, dst, ss, rs, device_id=to, device_id_type=MESH)

    z_dev = dev(zl, y, c, x, 1 - zh)
    sib = dev(zl, y, 1 - c, x, zh)
    owner = c == zh

    barrier = pltpu.get_barrier_semaphore()
    for dx in (1, 3, 2):
        pl.semaphore_signal(barrier, inc=1, device_id=dev(zl, y, c, (x + dx) % 4, zh), device_id_type=MESH)

    for d in range(63, 0, -1):
        to = dev((zl + d // 16) % 4, (y + (d // 4) % 4) % 4, (c + d % 2) % 2, x, (zh + (d // 2) % 2) % 2)
        pl.semaphore_signal(barrier, inc=1, device_id=to, device_id_type=MESH)

    half_cols = XCOLS // 2
    parts = ((q_hbm, qx, 0, XCOLS), (k_hbm, kx, 0, XCOLS), (v_hbm, vx, 0, half_cols), (v_hbm, vx, half_cols, half_cols))

    def a_from(t, xp):
        src, _, lo, n = parts[t]
        return src.at[:, pl.ds(pl.multiple_of(xp * XCOLS + lo, 128), n)]

    def a_to(t):
        _, dst, lo, n = parts[t]
        return dst.at[pl.ds(aligned(x, TOK), TOK), pl.ds(lo, n)]

    def a_copy(t, dx):
        xp = (x + dx) % 4
        return remote(a_from(t, xp), a_to(t), a_send.at[t, dx], a_recv.at[t, dx], dev(zl, y, c, xp, zh))

    def a_local(t):
        return pltpu.make_async_copy(a_from(t, x), a_to(t), a_loc.at[t])

    def a_wait(t):
        for dx in (1, 3, 2):
            a_copy(t, dx).wait_recv()
        a_local(t).wait()

    edge = jnp.logical_or(zl == 0, zl == 3)
    away = jnp.logical_not(owner)

    def piece(y_, p):
        return ws.at[pl.ds(pl.multiple_of(y_ * 768 + p * 128, 128), 128), :]

    def w1_copy(p):
        return remote(piece(y, p), piece(y, p), w1_send.at[p], w1_recv.at[p], dev(3 - zl, y, c, x, 1 - zh))

    def wi_copy(p):
        to = dev(1 + zl // 3, y, c, x, zh)
        return remote(piece(y, p), piece(y, p), wi_send.at[p], w1_recv.at[p], to)

    def w2_copy(p, dy):
        to = dev(zl, (y + dy) % 4, c, x, zh)
        return remote(piece(y, p), piece(y, p), w2_send.at[p, dy], w2_recv.at[p, dy], to)

    def w_forward(outer, inner):
        def some(pieces, behind):
            for p in pieces:
                w1_copy(p).wait_recv()
                if behind:
                    wi_copy(p).start()
                for dy in (1, 3, 2):
                    w2_copy(p, dy).start()

        if outer:

            @pl.when(jnp.logical_and(away, edge))
            def _():
                some(outer, True)

        if inner:

            @pl.when(jnp.logical_and(away, jnp.logical_not(edge)))
            def _():
                some(inner, False)

    def w_scale(first, last):
        @pl.loop(first, last)
        def _(i):
            kc = (y * 6 + i) % 24
            g = jnp.broadcast_to(gain[pl.ds(kc, 1), :], (128, 128)).T
            rows = pl.ds(aligned(kc, 128), 128)
            for i in range(3):
                for j in range(NHEADS):
                    scaled = wv[i, rows, j * HEAD : (j + 1) * HEAD].astype(F32) * g
                    ws[rows, i * NCOLS + j * HEAD : i * NCOLS + (j + 1) * HEAD] = scaled.astype(BF16)

    for t in range(4):
        a_local(t).start()

    @pl.when(owner)
    def _():
        load = pltpu.make_async_copy(w_hbm, wv, w_loc)
        load.start()
        load.wait()
        w_scale(0, 6)

    pl.semaphore_wait(barrier, 66)
    for t in range(4):
        for dx in (1, 3, 2):
            a_copy(t, dx).start()

    @pl.when(jnp.logical_and(owner, edge))
    def _():
        for p in range(6):
            w1_copy(p).start()

    @pl.when(owner)
    def _():
        w_scale(6, 24)

    w_forward((0, 1), ())
    a_wait(0)
    pool = (
        lax.broadcasted_iota(jnp.int32, (64, HALF_TOK), 1) // 8 == lax.broadcasted_iota(jnp.int32, (64, HALF_TOK), 0)
    ).astype(F32) * 0.125
    ag[zh] = jnp.dot(pool.astype(BF16), qx[...], preferred_element_type=F32).astype(BF16)
    ag_copy = remote(ag.at[zh], ag.at[zh], z_send.at[0], z_recv.at[0], z_dev)
    ag_copy.start()
    w_forward((2, 3), (0,))
    ag_copy.wait_recv()
    w_forward((4, 5), (1, 2))

    def nt(a, b):
        return lax.dot_general(a, b, (((1,), (1,)), ((), ())), preferred_element_type=F32)

    def head(h):
        return slice(h * HEAD, (h + 1) * HEAD)

    def agents(h):
        return ag[:, :, head(h)].reshape(2 * 64, HEAD)

    for h in range(XHEADS):
        s = nt(qx[:, head(h)], agents(h)) * SCALE
        e = jnp.exp(s - jnp.max(s, axis=1, keepdims=True))
        tw[h] = e * (1.0 / jnp.sum(e, axis=1, keepdims=True))
    w_forward((), (3,))

    a_wait(1)
    lane = lax.broadcasted_iota(jnp.int32, (128, 128), 1)
    stats = jnp.where(lane < 8, 0.0, 1.0)
    for h in range(XHEADS):
        s = nt(agents(h), kx[:, head(h)]) * SCALE
        m = jnp.max(s, axis=1, keepdims=True)
        e = jnp.exp(s - m)
        pb[h] = e.astype(BF16)
        stats = jnp.where(lane == h, m, stats)
        stats = jnp.where(lane == 8 + h, jnp.sum(e, axis=1, keepdims=True), stats)
    st[zh] = stats.T[0:16, :]
    st_copy = remote(st.at[zh], st.at[zh], z_send.at[1], z_recv.at[1], z_dev)
    st_copy.start()
    w_forward((), (4, 5))

    def nb_copy(i):
        half = nb.at[zh, 3 * i : 3 * i + 3]
        return remote(half, half, z_send.at[2 + i], z_recv.at[2 + i], z_dev)

    for i in range(2):
        a_wait(2 + i)
        for h in range(3 * i, 3 * i + 3):
            nb[zh, h] = jnp.dot(pb[h], vx[:, head(h)], preferred_element_type=F32).astype(BF16)
        nb_copy(i).start()
    st_copy.wait_recv()
    m0, m1 = st[0, 0:8, :], st[1, 0:8, :]
    l0, l1 = st[0, 8:16, :], st[1, 8:16, :]
    peak = jnp.maximum(m0, m1)
    e0, e1 = jnp.exp(m0 - peak), jnp.exp(m1 - peak)
    inv = 1.0 / (l0 * e0 + l1 * e1)
    s0, s1 = e0 * inv, e1 * inv

    for h in range(XHEADS):
        if h % 3 == 0:
            nb_copy(h // 3).wait_recv()
        t = tw[h]
        both = jnp.concatenate([(t * s0[h : h + 1, :]).astype(BF16), (t * s1[h : h + 1, :]).astype(BF16)], axis=1)
        sb[:, head(h)] = jnp.dot(
            both, nb[:, h].reshape(256, HEAD), preferred_element_type=F32
        ).astype(BF16)

    z = zh * 4 + zl
    me = z * 4 + y

    def nearest(step):
        return (step % 2) * ((step + 1) // 2) + (1 - step % 2) * ((8 - step // 2) % 8)

    def b_copy(n):
        z_, y_ = (z + nearest(n // 4)) % 8, (y + n % 4) % 4
        return remote(
            sb.at[pl.ds(aligned(y_ * 8 + z_, LOC), LOC), :],
            xb.at[c, x, pl.ds(aligned(me, LOC), LOC), :],
            b_send.at[n], b_recv.at[n], dev(z_ % 4, y_, c, x, z_ // 4),
        )

    def b_wait(n):
        z_, y_ = (z + 8 - nearest(n // 4)) % 8, (y + 4 - n % 4) % 4
        dst = xb.at[c, x, pl.ds(aligned(z_ * 4 + y_, LOC), LOC), :]
        remote(dst, dst, b_send.at[n], b_recv.at[n], z_dev).wait_recv()

    group = y * 8 + z
    own = pltpu.make_async_copy(
        sb.at[pl.ds(aligned(group, LOC), LOC), :], xb.at[c, x, pl.ds(aligned(me, LOC), LOC), :], b_loc
    )
    own.start()

    @pl.loop(1, 32)
    def _(n):
        b_copy(n).start()

    left, right, far = (x + 3) % 4, (x + 1) % 4, (x + 2) % 4

    def block(half, col, s, lo=0, n=64):
        z_ = (z + 8 - nearest(s)) % 8
        return xb.at[half, col, pl.ds(pl.multiple_of(z_ * 64 + lo, 32), n), :]

    def x_own(s, i):
        b = block(c, x, s)
        return remote(b, b, x_send.at[s, i], x_recv.at[s, i], dev(zl, y, c, (right, left)[i], zh))

    def x_fwd(s, i):
        b = block(c, (left, right)[i], s, 32 * i, 32)
        return remote(b, b, x_send.at[s, 2 + i], x_recv.at[s, 2 + i], dev(zl, y, c, (right, left)[i], zh))

    def x_got(s, i):
        col = (left, right, far, far)[i]
        b = block(c, col, s, *((0, 64), (0, 64), (0, 32), (32, 32))[i])
        return remote(b, b, x_send.at[s, i], x_recv.at[s, i], z_dev)

    def to_sib(s, i):
        b = block(c, (x, left, right, far)[i], s)
        return remote(b, b, s_send.at[s, i], s_recv.at[s, i], sib)

    def from_sib(s, i):
        b = block(1 - c, (x, left, right, far)[i], s)
        return remote(b, b, s_send.at[s, i], s_recv.at[s, i], sib)

    def mm(half, col, first=False):
        rows_w = pl.ds(aligned(col, XCOLS), XCOLS)

        @pl.loop(0, 2)
        def _(i):
            src = xb[half, col, pl.ds(aligned(i, 256), 256), :]
            p = jnp.dot(src, ws[rows_w, :], preferred_element_type=F32)
            wide = src.astype(F32)
            sq = jnp.broadcast_to(jnp.sum(wide * wide, axis=1, keepdims=True), (256, 128)).reshape(16, LOC, 128)
            for j in range(3 * NHEADS):
                pj = p[:, head(j)].reshape(16, LOC, 128)
                if first:
                    acc[j, half, i] = pj
                else:
                    acc[j, half, i] += pj
            if first:
                ssq[half, i] = sq
            else:
                ssq[half, i] += sq

    def sides(s):
        for i in range(2):
            x_got(s, i).wait_recv()
            x_fwd(s, i).start()
            to_sib(s, 1 + i).start()

    def ends(s):
        x_got(s, 2).wait_recv()
        x_got(s, 3).wait_recv()
        to_sib(s, 3).start()

    for s in range(8):
        if s == 0:
            own.wait()
        for n in range(4 * s, 4 * s + 4):
            if n:
                b_wait(n)
        x_own(s, 0).start()
        x_own(s, 1).start()
        to_sib(s, 0).start()
        if s >= 1:
            sides(s - 1)
        if s >= 2:
            ends(s - 2)

    @pl.when(away)
    def _():
        for p in range(6):
            for dy in (1, 3, 2):
                dst = piece((y + 4 - dy) % 4, p)
                remote(dst, dst, w2_send.at[p, dy], w2_recv.at[p, dy], z_dev).wait_recv()

    mm(c, x, True)
    for s in range(8):
        from_sib(s, 0).wait_recv()
    mm(1 - c, x, True)
    sides(7)
    ends(6)
    mm(c, left)
    mm(c, right)
    for s in range(8):
        from_sib(s, 1).wait_recv()
        from_sib(s, 2).wait_recv()
    mm(1 - c, left)
    ends(7)
    mm(1 - c, right)
    mm(c, far)
    for s in range(8):
        from_sib(s, 3).wait_recv()
    mm(1 - c, far)
    ssq[...] = lax.rsqrt(ssq[...] * (1.0 / D) + EPS)

    same = lax.broadcasted_iota(jnp.int32, (256, 256), 0) % 8 == lax.broadcasted_iota(jnp.int32, (256, 256), 1) % 8

    def attend(zh_, lo):
        norm = ssq[:, zh_, :, lo : lo + 8, :].reshape(256, 128)

        def rows_of(j):
            return (acc[j, :, zh_, :, lo : lo + 8, :].reshape(256, 128) * norm).astype(BF16)

        for h in range(NHEADS):
            s = nt(rows_of(h), rows_of(NHEADS + h)) * SCALE
            s = jnp.where(same, s, -1e30)
            e = jnp.exp(s - jnp.max(s, axis=1, keepdims=True))
            p = (e * (1.0 / jnp.sum(e, axis=1, keepdims=True))).astype(BF16)
            o = jnp.dot(p, rows_of(2 * NHEADS + h), preferred_element_type=F32)
            ob[:, zh_, :, lo : lo + 8, head(h)] = o.astype(BF16).reshape(2, 16, 8, HEAD)

    def c_to(g, c_):
        return rb.at[pl.ds(aligned(g, LOC), LOC), pl.ds(aligned(c_, NCOLS), NCOLS)]

    def c_copy(d, hs):
        zl_, y_, c_, zh_ = (zl + d // 8) % 4, (y + (d // 2) % 4) % 4, (c + d % 2) % 2, (zh + hs) % 2
        src = ob.at[c_, zh_, zl_ * 4 + y_]
        return remote(src, c_to(group, c), c_send.at[hs, d], c_recv.at[hs, d], dev(zl_, y_, c_, x, zh_))

    def c_own():
        return pltpu.make_async_copy(ob.at[c, zh, zl * 4 + y], c_to(group, c), c_loc)

    for hs in (1, 0):
        for lo in (0, 8):
            attend((zh + hs) % 2, lo)

        @pl.loop(1 - hs, 32)
        def _(d):
            c_copy(d, hs).start()

    c_own().start()

    def c_wait(z_, y_, dc):
        d = ((zl + 4 - z_ % 4) % 4) * 8 + ((y + 4 - y_) % 4) * 2 + dc
        hs = (zh + z_ // 4) % 2
        dst = c_to(y_ * 8 + z_, (c + dc) % 2)

        @pl.when(d + hs > 0)
        def _():
            remote(dst, dst, c_send.at[hs, d], c_recv.at[hs, d], z_dev).wait_recv()

        @pl.when(d + hs == 0)
        def _():
            c_own().wait()

    def o_copy(s, dx):
        z_, xp = (z + 8 - nearest(s)) % 8, (x + dx) % 4
        return remote(
            rb.at[pl.ds(aligned(xp * 8 + z_, LOC), LOC), :],
            out.at[pl.ds(aligned(z_, LOC), LOC), pl.ds(aligned(x, XCOLS), XCOLS)],
            o_send.at[s, dx], o_recv.at[s, dx], dev(zl, y, c, xp, zh),
        )

    @pl.loop(0, 8)
    def _(s):
        z_ = (z + 8 - nearest(s)) % 8
        for dx in (1, 3, 2, 0):
            for dc in range(2):
                c_wait(z_, (x + dx) % 4, dc)
            if dx:
                o_copy(s, dx).start()

    mine = pltpu.make_async_copy(
        rb.at[pl.ds(aligned(x, TOK), TOK), :], out.at[:, pl.ds(aligned(x, XCOLS), XCOLS)], o_loc
    )
    mine.start()

    for t in range(4):
        for dx in (1, 3, 2):
            a_copy(t, dx).wait_send()

    @pl.when(jnp.logical_and(owner, edge))
    def _():
        for p in range(6):
            w1_copy(p).wait_send()

    @pl.when(jnp.logical_and(away, edge))
    def _():
        for p in range(6):
            wi_copy(p).wait_send()

    @pl.when(away)
    def _():
        for p in range(6):
            for dy in (1, 3, 2):
                w2_copy(p, dy).wait_send()

    ag_copy.wait_send()
    st_copy.wait_send()
    for i in range(2):
        nb_copy(i).wait_send()

    @pl.loop(1, 32)
    def _(d):
        b_copy(d).wait_send()

    for s in range(8):
        for i in range(2):
            x_own(s, i).wait_send()
            x_fwd(s, i).wait_send()
        for i in range(4):
            to_sib(s, i).wait_send()

    @pl.loop(1, 64)
    def _(d):
        c_copy(d % 32, d // 32).wait_send()

    mine.wait()

    @pl.loop(0, 8)
    def _(s):
        for dx in (1, 3, 2):
            o_copy(s, dx).wait_send()

    @pl.loop(0, 8)
    def _(s):
        z_ = (z + 8 - nearest(s)) % 8
        for dx in (1, 3, 2):
            dst = out.at[pl.ds(aligned(z_, LOC), LOC), pl.ds(aligned((x + 4 - dx) % 4, XCOLS), XCOLS)]
            src = rb.at[pl.ds(0, LOC), :]
            remote(src, dst, o_send.at[s, dx], o_recv.at[s, dx], z_dev).wait_recv()


def local(spatial_q, spatial_k, spatial_v, norm_gain, temporal_weight):
    dma = pltpu.SemaphoreType.DMA
    flat = [a.reshape(TOK, D) for a in (spatial_q, spatial_k, spatial_v)]
    hbm = pl.BlockSpec(memory_space=pl.ANY)
    out = pl.pallas_call(
        kernel,
        out_shape=jax.ShapeDtypeStruct((TOK, D), BF16),
        in_specs=[hbm, hbm, hbm, pl.BlockSpec(memory_space=pltpu.VMEM), hbm],
        out_specs=hbm,
        scratch_shapes=[
            pltpu.VMEM((HALF_TOK, XCOLS), BF16),
            pltpu.VMEM((HALF_TOK, XCOLS), BF16),
            pltpu.VMEM((HALF_TOK, XCOLS), BF16),
            pltpu.VMEM((2, 64, XCOLS), BF16),
            pltpu.VMEM((XHEADS, HALF_TOK, 128), F32),
            pltpu.VMEM((XHEADS, 128, HALF_TOK), BF16),
            pltpu.VMEM((2, XHEADS, 128, HEAD), BF16),
            pltpu.VMEM((2, 16, 128), F32),
            pltpu.VMEM((HALF_TOK, XCOLS), BF16),
            pltpu.VMEM((3, D, NCOLS), BF16),
            pltpu.VMEM((D, 3 * NCOLS), BF16),
            pltpu.VMEM((2, 4, HALF_TOK, XCOLS), BF16),
            pltpu.VMEM((3 * NHEADS, 2, 2, 16, LOC, HEAD), F32),
            pltpu.VMEM((2, 2, 16, LOC, 128), F32),
            pltpu.VMEM((2, 2, 16, LOC, NCOLS), BF16),
            pltpu.VMEM((HALF_TOK, XCOLS), BF16),
            dma((4, 4)), dma((4, 4)), dma((4,)),
            dma((4,)), dma((4,)),
            dma, dma((6,)), dma((6,)), dma((6,)), dma((6, 4)), dma((6, 4)),
            dma((32,)), dma((32,)), dma,
            dma((8, 4)), dma((8, 4)),
            dma((8, 4)), dma((8, 4)),
            dma((2, 32)), dma((2, 32)), dma,
            dma((8, 4)), dma((8, 4)), dma,
        ],
        compiler_params=pltpu.CompilerParams(collective_id=0, has_side_effects=True, vmem_limit_bytes=56 << 20),
    )(*flat, norm_gain.reshape(D // 128, 128), temporal_weight.transpose(1, 0, 2))
    return out.reshape(1, TOK, D)


def solution(mesh):
    return jax.shard_map(
        local,
        mesh=mesh,
        in_specs=(
            P("frame", "row", None),
            P("frame", "row", None),
            P("frame", "row", None),
            P(),
            P(None, None, "row"),
        ),
        out_specs=P("frame", "row", None),
        check_vma=False,
    )
```

time: 148 us -> 138 us (0.932)
  the two profiles are of different devices: /device:TPU:194 before, /device:TPU:226 now
where the time goes in v3:
time: 138 us
  Pallas kernels  136 us (99%)
  local copies, waits for them, and re-layouts  2.06 us (1%)
    pallas_call x1, Pallas kernels, local(): pl.pallas_call(kernel, out_shape=jax.ShapeDtypeStruct((TOK, D), BF16), in...  136 us

profile of v3, /device:TPU:226, one launch (start us, length us, event | category | flops | bytes accessed | tf_op | source)
XLA Modules:
  0.0 137.6 jit_solution(7459470630703878070)
XLA Ops:
  0.0 135.6 %shard_map.55 = bf16[128,3072]{1,0:T(8,128)(2,1)} custom-call(bf16[128,3072]{1,0:T(8,128)(2,1)} %bitcast.8, bf16[128,3072]{1,0:T(8,128)(2,1)} %bitcast.9, bf16[128,3072]{1,0:T(8,128)(2,1)} %bitcast.10, f32[24,128]{1,0:T(8,128)} %bitcast.11, bf16[3,3072,384]{2,1,0:T(8,128)(2,1)} %bitcast.6), custom_call_target="tpu_custom_call" | custom-call | tf_op jit(solution)/shard_map/pallas_call | solution.py:481
  135.6 2.1 %copy.7 = bf16[1,128,3072]{2,1,0:T(8,128)(2,1)} copy(bf16[1,128,3072]{2,1,0:T(8,128)(2,1)} %bitcast.7) | data formatting | bytes 1572864

commit v4 on v3

--- a/solution.py
+++ b/solution.py
@@ -160,7 +160,6 @@
     ag_copy.start()
     w_forward((2, 3), (0,))
     ag_copy.wait_recv()
-    w_forward((4, 5), (1, 2))
 
     def nt(a, b):
         return lax.dot_general(a, b, (((1,), (1,)), ((), ())), preferred_element_type=F32)
@@ -175,7 +174,7 @@
         s = nt(qx[:, head(h)], agents(h)) * SCALE
         e = jnp.exp(s - jnp.max(s, axis=1, keepdims=True))
         tw[h] = e * (1.0 / jnp.sum(e, axis=1, keepdims=True))
-    w_forward((), (3,))
+    w_forward((4,), (1, 2))
 
     a_wait(1)
     lane = lax.broadcasted_iota(jnp.int32, (128, 128), 1)
@@ -190,7 +189,7 @@
     st[zh] = stats.T[0:16, :]
     st_copy = remote(st.at[zh], st.at[zh], z_send.at[1], z_recv.at[1], z_dev)
     st_copy.start()
-    w_forward((), (4, 5))
+    w_forward((5,), (3,))
 
     def nb_copy(i):
         half = nb.at[zh, 3 * i : 3 * i + 3]
@@ -201,6 +200,7 @@
         for h in range(3 * i, 3 * i + 3):
             nb[zh, h] = jnp.dot(pb[h], vx[:, head(h)], preferred_element_type=F32).astype(BF16)
         nb_copy(i).start()
+    w_forward((), (4, 5))
     st_copy.wait_recv()
     m0, m1 = st[0, 0:8, :], st[1, 0:8, :]
     l0, l1 = st[0, 8:16, :], st[1, 8:16, :]
@@ -243,9 +243,12 @@
     )
     own.start()
 
-    @pl.loop(1, 32)
-    def _(n):
-        b_copy(n).start()
+    def b_start(first, last):
+        @pl.loop(first, last)
+        def _(n):
+            b_copy(n).start()
+
+    b_start(1, 20)
 
     left, right, far = (x + 3) % 4, (x + 1) % 4, (x + 2) % 4
 
@@ -311,6 +314,8 @@
         for n in range(4 * s, 4 * s + 4):
             if n:
                 b_wait(n)
+        if s < 3:
+            b_start(4 * s + 20, 4 * s + 24)
         x_own(s, 0).start()
         x_own(s, 1).start()
         to_sib(s, 0).start()

time: 138 us -> 137 us (level)
  the two profiles are of different devices: /device:TPU:226 before, /device:TPU:130 now
where the time goes in v4:
time: 137 us; the launch traced here: 136 us
  Pallas kernels  134 us (98%)
  local copies, waits for them, and re-layouts  2.06 us (2%)
    pallas_call x1, Pallas kernels, local(): pl.pallas_call(kernel, out_shape=jax.ShapeDtypeStruct((TOK, D), BF16), in...  134 us

profile of v4, /device:TPU:130, one launch (start us, length us, event | category | flops | bytes accessed | tf_op | source)
XLA Modules:
  0.0 136.3 jit_solution(9147914299738064100)
XLA Ops:
  0.0 134.3 %shard_map.55 = bf16[128,3072]{1,0:T(8,128)(2,1)} custom-call(bf16[128,3072]{1,0:T(8,128)(2,1)} %bitcast.8, bf16[128,3072]{1,0:T(8,128)(2,1)} %bitcast.9, bf16[128,3072]{1,0:T(8,128)(2,1)} %bitcast.10, f32[24,128]{1,0:T(8,128)} %bitcast.11, bf16[3,3072,384]{2,1,0:T(8,128)(2,1)} %bitcast.6), custom_call_target="tpu_custom_call" | custom-call | tf_op jit(solution)/shard_map/pallas_call | solution.py:486
  134.3 2.1 %copy.7 = bf16[1,128,3072]{2,1,0:T(8,128)(2,1)} copy(bf16[1,128,3072]{2,1,0:T(8,128)(2,1)} %bitcast.7) | data formatting | bytes 1572864
